TPU v7x, 128 devices: a whole 4x4x4 slice. The times are simulated.
128 devices in a mesh: fsdp: 16 (over z, x_lo, core), tp: 8 (over x_hi, y).
Axes of the slice: x: 4 (x_hi: 2, x_lo: 2; x = x_hi * 2 + x_lo), y: 4, z: 4, core: 2. Of those that a mesh axis runs over, the one named last changes fastest.
Arguments:
- states: bfloat16 [512, 4, 8192], P('fsdp'), may hold values from -6 to 6
- norm_gain: float32 [8192], replicated, may hold values from 0.5 to 1.5
- query_base: bfloat16 [8192, 8192], P(('fsdp', 'tp')), may hold values from -0.0625 to 0.0625
- key_base: bfloat16 [8192, 1024], P(('fsdp', 'tp')), may hold values from -0.0625 to 0.0625
- value_base: bfloat16 [8192, 1024], P(('fsdp', 'tp')), may hold values from -0.0625 to 0.0625
- output_base: bfloat16 [8192, 8192], P(('fsdp', 'tp')), may hold values from -0.5 to 0.5
- query_down: bfloat16 [4, 8192, 64], P(None, ('fsdp', 'tp')), may hold values from -0.0625 to 0.0625
- query_up: bfloat16 [4, 64, 8192], replicated, may hold values from -0.75 to 0.75
- key_down: bfloat16 [4, 8192, 64], P(None, ('fsdp', 'tp')), may hold values from -0.0625 to 0.0625
- key_up: bfloat16 [4, 64, 1024], replicated, may hold values from -0.75 to 0.75
- value_down: bfloat16 [4, 8192, 64], P(None, ('fsdp', 'tp')), may hold values from -0.0625 to 0.0625
- value_up: bfloat16 [4, 64, 1024], replicated, may hold values from -0.75 to 0.75
- output_down: bfloat16 [4, 8192, 64], P(None, ('fsdp', 'tp')), may hold values from -0.5 to 0.5
- output_up: bfloat16 [4, 64, 8192], replicated, may hold values from -0.75 to 0.75
- adapter_layer: int32 [1], replicated, may hold values from 0 to 3
- kv_lengths: int32 [512], P('fsdp'), may hold values from 8 to 512
- cache_keys: bfloat16 [512, 512, 8, 128], P('fsdp', None, 'tp'), may hold values from -320 to 320
- cache_values: bfloat16 [512, 512, 8, 128], P('fsdp', None, 'tp'), may hold values from -6 to 6
Outputs:
- layer_update: bfloat16 [512, 4, 8192], P('fsdp', None, 'tp')
Inputs may be any that keep to these rules, and one draw needn't show every extreme that they name: `kv_lengths`: slots at and beyond a sequence's length hold no cached position.
All inputs are finite; a program needn't handle non-finite values.
Results may differ from a plain program's by a relative error of at most 0.012.
The roundings to bfloat16 on the way count: a program that leaves them out, or rounds other values in their place, can miss the bound.
Values may be sent and summed in bfloat16 or wider, within the bound.
A program may use at most 128 MiB of HBM per device.

v0:
```python
import jax
import jax.numpy as jnp
from jax import lax
from jax.sharding import PartitionSpec as P

HQ = 64
KVH = 8
DH = 128
rope_theta = 1000000.0
low_rank_scale = 0.5
epsilon = 1e-06


def sent_to_all(array, axis):
    copies = jnp.broadcast_to(array, (lax.axis_size(axis), *array.shape))
    return lax.all_to_all(copies, axis, split_axis=0, concat_axis=0, tiled=True)


def joined_along(tiles, dim):
    tiles = jnp.moveaxis(tiles, 0, dim)
    shape = tiles.shape
    return tiles.reshape(*shape[:dim], shape[dim] * shape[dim + 1], *shape[dim + 2 :])


def collect(array, axis, dim):
    tiles = sent_to_all(array, axis)
    return joined_along(tiles, dim)


def merge_rows(frozen_base_rows, down_stack, up_stack, adapter_slot):
    down_rows = lax.dynamic_index_in_dim(down_stack, adapter_slot, 0, keepdims=False)
    up_projection_rows = lax.dynamic_index_in_dim(up_stack, adapter_slot, 0, keepdims=False)
    low_rank_delta = jnp.dot(down_rows, up_projection_rows, preferred_element_type=jnp.float32)
    return (frozen_base_rows.astype(jnp.float32) + low_rank_scale * low_rank_delta).astype(
        jnp.bfloat16
    )


def normalize(states, norm_gain):
    widened = states.astype(jnp.float32)
    squared_average = jnp.mean(widened * widened, axis=-1, keepdims=True)
    return (widened * lax.rsqrt(squared_average + epsilon) * norm_gain).astype(jnp.bfloat16)


def rotate(vectors, positions):
    head_dim = vectors.shape[-1]
    half_dim = head_dim // 2
    frequency = rope_theta ** (-2.0 * jnp.arange(half_dim, dtype=jnp.float32) / head_dim)
    rotation_phases = positions[:, :, None] * frequency[None, None, :]
    cosine_table = jnp.concatenate((jnp.cos(rotation_phases), jnp.cos(rotation_phases)), -1)[
        :, :, None, :
    ]
    sine_table = jnp.concatenate((jnp.sin(rotation_phases), jnp.sin(rotation_phases)), -1)[
        :, :, None, :
    ]
    turned = jnp.concatenate((-vectors[..., half_dim:], vectors[..., :half_dim]), -1)
    return vectors * cosine_table + turned * sine_table


def attend(queries, keys_new, values_new, cache_k, cache_v, lengths):
    seq_count, step_count, head_count, head_dim = queries.shape
    kv_count = keys_new.shape[2]
    grouped = queries.reshape(seq_count, step_count, kv_count, head_count // kv_count, head_dim)
    score_scale = head_dim ** (-0.5)
    old_scores = (
        jnp.einsum("bskgd,blkd->bskgl", grouped, cache_k, preferred_element_type=jnp.float32)
        * score_scale
    )
    new_scores = (
        jnp.einsum("bskgd,btkd->bskgt", grouped, keys_new, preferred_element_type=jnp.float32)
        * score_scale
    )
    live_slots = jnp.arange(cache_k.shape[1], dtype=jnp.int32)[None, :] < lengths[:, None]
    old_scores = jnp.where(live_slots[:, None, None, None, :], old_scores, -1e30)
    causal = jnp.arange(step_count)[:, None] >= jnp.arange(step_count)[None, :]
    new_scores = jnp.where(causal[None, :, None, None, :], new_scores, -1e30)
    highest = jnp.maximum(jnp.max(old_scores, -1), jnp.max(new_scores, -1))[..., None]
    old_exp = jnp.exp(old_scores - highest)
    new_exp = jnp.exp(new_scores - highest)
    denominator = jnp.sum(old_exp, -1, keepdims=True) + jnp.sum(new_exp, -1, keepdims=True)
    old_weights = (old_exp / denominator).astype(jnp.bfloat16)
    new_weights = (new_exp / denominator).astype(jnp.bfloat16)
    mixture = jnp.einsum(
        "bskgl,blkd->bskgd", old_weights, cache_v, preferred_element_type=jnp.float32
    )
    mixture = mixture + jnp.einsum(
        "bskgt,btkd->bskgd", new_weights, values_new, preferred_element_type=jnp.float32
    )
    return mixture.astype(jnp.bfloat16).reshape(seq_count, step_count, head_count * head_dim)


def local(
    states,
    norm_gain,
    query_base,
    key_base,
    value_base,
    output_base,
    query_down,
    query_up,
    key_down,
    key_up,
    value_down,
    value_up,
    output_down,
    output_up,
    adapter_layer,
    kv_lengths,
    cache_keys,
    cache_values,
):
    adapter_slot = adapter_layer[0]
    tp_size = lax.axis_size("tp")
    row_count = query_base.shape[0]
    merged_query = merge_rows(query_base, query_down, query_up, adapter_slot)
    merged_key = merge_rows(key_base, key_down, key_up, adapter_slot)
    merged_value = merge_rows(value_base, value_down, value_up, adapter_slot)
    merged_output = merge_rows(output_base, output_down, output_up, adapter_slot)
    joined = jnp.concatenate(
        (
            merged_query.reshape(row_count, tp_size, -1),
            merged_key.reshape(row_count, tp_size, -1),
            merged_value.reshape(row_count, tp_size, -1),
        ),
        2,
    ).reshape(row_count, -1)
    input_slice, output_slice = (
        lax.all_to_all(joined, "tp", split_axis=1, concat_axis=0, tiled=True),
        lax.all_to_all(merged_output, "tp", split_axis=1, concat_axis=0, tiled=True),
    )
    seq_count, step_count, model_width = states.shape
    normed = normalize(states, norm_gain)
    head_cols = HQ * DH // tp_size
    kv_cols = KVH * DH // tp_size
    flat_rows = normed.reshape(seq_count * step_count, model_width)
    columns = flat_rows
    projected = jnp.dot(
        columns,
        lax.all_gather(input_slice, "fsdp", axis=0, tiled=True),
        preferred_element_type=jnp.float32,
    )
    projected = projected.reshape(seq_count, step_count, -1)
    positions = (
        kv_lengths.astype(jnp.float32)[:, None] + jnp.arange(step_count, dtype=jnp.float32)[None, :]
    )
    queries = rotate(
        projected[:, :, :head_cols].reshape(seq_count, step_count, -1, DH), positions
    ).astype(jnp.bfloat16)
    keys_new = rotate(
        projected[:, :, head_cols : head_cols + kv_cols].reshape(seq_count, step_count, -1, DH),
        positions,
    ).astype(jnp.bfloat16)
    values_new = (
        projected[:, :, head_cols + kv_cols :]
        .reshape(seq_count, step_count, -1, DH)
        .astype(jnp.bfloat16)
    )
    attended = attend(queries, keys_new, values_new, cache_keys, cache_values, kv_lengths)
    all_heads = collect(attended, "tp", 2)
    flat_heads = all_heads.reshape(seq_count * step_count, -1)
    columns = flat_heads
    low_rank_delta = jnp.dot(
        columns,
        lax.all_gather(output_slice, "fsdp", axis=0, tiled=True),
        preferred_element_type=jnp.float32,
    )
    low_rank_delta = low_rank_delta.reshape(seq_count, step_count, -1)
    return low_rank_delta.astype(jnp.bfloat16)


def solution(mesh):
    in_specs = (
        P("fsdp", None, None),
        P(),
        P(("fsdp", "tp"), None),
        P(("fsdp", "tp"), None),
        P(("fsdp", "tp"), None),
        P(("fsdp", "tp"), None),
        P(None, ("fsdp", "tp"), None),
        P(),
        P(None, ("fsdp", "tp"), None),
        P(),
        P(None, ("fsdp", "tp"), None),
        P(),
        P(None, ("fsdp", "tp"), None),
        P(),
        P(),
        P("fsdp"),
        P("fsdp", None, "tp", None),
        P("fsdp", None, "tp", None),
    )
    out_specs = P("fsdp", None, "tp")
    return jax.shard_map(local, mesh=mesh, in_specs=in_specs, out_specs=out_specs, check_vma=False)
```

profile of v0, /device:TPU:1, one launch (start us, length us, event | category | flops | bytes accessed | tf_op | source)
XLA Modules:
  0.0 290.6 jit_solution(4913275454677924409)
XLA Ops:
  6.5 0.0 copy-start
  6.5 0.0 all-gather.3.cloned.1.call-start
  7.3 0.0 copy-start.6
  7.3 2.0 fusion.7
  9.3 0.1 copy.110
  9.4 0.9 fusion.33
  10.3 1.1 fusion.34
  11.4 0.1 copy_bitcast_fusion.2
  11.5 0.1 pad_maximum_fusion
  11.6 0.0 copy-start.5
  11.6 26.0 %all_to_all.40 = bf16[64,8,1280]{2,0,1:T(8,128)(2,1)} all-to-all(bf16[64,8,1280]{2,0,1:T(8,128)(2,1)S(1)} %pad_maximum_fusion), channel_id=1, replica_groups=mesh['fsdp'=16,'tp'=8] {'tp'}, dimensions={1} | all-to-all | bytes 2621440 | tf_op jit(solution)/shard_map/all_to_all | solution.py:128
  37.6 0.0 all-gather.3.cloned.1.call-update
  37.6 0.0 all-gather.5.cloned.1.call-start
  37.7 1.7 fusion.6
  39.3 0.1 copy.109
  39.4 0.0 copy-start.9
  39.4 0.0 copy-start.2
  39.4 21.3 %all_to_all.41 = bf16[64,8,1024]{2,0,1:T(8,128)(2,1)} all-to-all(bf16[64,8,1024]{2,0,1:T(8,128)(2,1)S(1)} %bitcast.136), channel_id=1, replica_groups=mesh['fsdp'=16,'tp'=8] {'tp'}, dimensions={1} | all-to-all | bytes 2097152 | tf_op jit(solution)/shard_map/all_to_all | solution.py:129
  60.7 0.0 all-gather.5.cloned.1.call-update
  60.8 0.0 copy-start.3
  60.8 0.1 iota_compare_fusion
  60.9 0.0 copy-done.2
  60.9 1.2 fusion.8
  62.1 0.3 multiply_cosine_fusion
  62.5 1.5 fusion.10
  63.9 92.0 %all-gather.3.cloned.1.call-done = bf16[8192,1280]{1,0:T(8,128)(2,1)} async-done(((bf16[512,1280]{1,0:T(8,128)(2,1)}), bf16[8192,1280]{1,0:T(8,128)(2,1)}) %all-gather.3.cloned.1.call-update) | async-done | bytes 20971536 | tf_op jit(solution)/shard_map/all_gather | solution.py:139
  155.9 11.4 %fusion = f32[32,4,1280]{2,0,1:T(8,128)S(1)} fusion(bf16[8192,1280]{1,0:T(8,128)(2,1)} %all-gather.3.cloned.1.call-done, bf16[32,4,8192]{2,1,0:T(4,128)(2,1)S(1)} %fusion.10), kind=kOutput, calls=%fused_computation | convolution fusion | flops 2684354560 | bytes 23724032 | tf_op jit(solution)/shard_map/dot_general | solution.py:137
  167.3 0.1 fusion.51
  167.4 0.1 fusion.54
  167.7 0.1 copy.92
  167.8 0.0 copy-start.4
  167.8 0.2 slice_negate_fusion
  168.0 0.2 fusion.43
  168.2 1.3 fusion.71
  169.5 0.4 copy-done.4
  170.0 1.6 fusion.70
  171.5 0.3 fusion.44
  171.8 0.8 fusion.17
  172.6 0.8 fusion.20
  173.5 0.4 fusion.27
  173.8 0.1 reshape.196
  173.9 0.1 copy.75
  174.0 0.3 broadcast_in_dim.26
  174.3 57.7 %all_to_all.42 = bf16[8,32,4,1024]{3,1,2,0:T(8,128)(2,1)S(1)} all-to-all(bf16[8,32,4,1024]{3,1,2,0:T(8,128)(2,1)S(1)} %broadcast_in_dim.26), channel_id=1, replica_groups=mesh['fsdp'=16,'tp'=8] {'tp'}, dimensions={0} | all-to-all | bytes 4194304 | tf_op jit(solution)/shard_map/all_to_all | solution.py:16
  232.0 0.2 copy.91
  232.1 42.5 %all-gather.5.cloned.1.call-done = bf16[8192,1024]{1,0:T(8,128)(2,1)} async-done(((bf16[512,1024]{1,0:T(8,128)(2,1)}), bf16[8192,1024]{1,0:T(8,128)(2,1)}) %all-gather.5.cloned.1.call-update) | async-done | bytes 16777232 | tf_op jit(solution)/shard_map/all_gather | solution.py:164
  274.6 8.2 %fusion.24 = bf16[32,4,1024]{2,0,1:T(8,128)(2,1)S(1)} fusion(bf16[32,4,8192]{2,0,1:T(8,128)(2,1)S(1)} %bitcast.128, bf16[8192,1024]{1,0:T(8,128)(2,1)} %all-gather.5.cloned.1.call-done), kind=kOutput, calls=%fused_computation.29 | convolution fusion | flops 2147614720 | bytes 19136512 | tf_op jit(solution)/shard_map/dot_general | solution.py:162
  282.8 0.9 copy.78
  (25 shorter events, 0.3 us)
Async XLA Ops:
  6.5 2.9 copy-start
  6.5 149.4 %all-gather.3.cloned.1.call-start = ((), (), s32[]{:S(2)}) async-start(), calls=%async_computation.3 | async-start | bytes 22282240 | tf_op jit(solution)/shard_map/all_gather | solution.py:139
  7.3 2.1 copy-start.6
  7.3 3.0 %copy-start.7 = (bf16[64,1024]{1,0:T(8,128)(2,1)S(1)}, bf16[64,1024]{1,0:T(8,128)(2,1)}, u32[]{:S(2)}) copy-start(bf16[64,1024]{1,0:T(8,128)(2,1)} %param.21) | copy-start | bytes 393220
  11.6 26.0 %copy-start.5 = (bf16[64,8192]{1,0:T(8,128)(2,1)S(1)}, bf16[64,8192]{1,0:T(8,128)(2,1)}, u32[]{:S(2)}) copy-start(bf16[64,8192]{1,0:T(8,128)(2,1)} %param.23) | copy-start | bytes 3145732
  37.6 237.0 %all-gather.5.cloned.1.call-start = ((), (), s32[]{:S(2)}) async-start(), calls=%async_computation.4 | async-start | bytes 17825792 | tf_op jit(solution)/shard_map/all_gather | solution.py:164
  39.4 21.3 %copy-start.9 = (s32[32]{0:T(128)S(1)}, s32[32]{0:T(128)}, u32[]{:S(2)}) copy-start(s32[32]{0:T(128)} %param.33) | copy-start | bytes 388
  39.4 21.5 %copy-start.2 = (bf16[32,4,8192]{2,1,0:T(4,128)(2,1)S(1)}, bf16[32,4,8192]{2,1,0:T(4,128)(2,1)}, u32[]{:S(2)}) copy-start(bf16[32,4,8192]{2,1,0:T(4,128)(2,1)} %param.18) | copy-start | bytes 6291460
  60.7 1.7 copy-start.8
  60.8 1.7 copy-start.3
  167.8 2.2 copy-start.4
  170.0 2.7 copy-start.10
  274.6 9.1 %copy-start.1 = (bf16[4,64,1024]{2,1,0:T(8,128)(2,1)S(1)}, bf16[4,64,1024]{2,1,0:T(8,128)(2,1)}, u32[]{:S(2)}) copy-start(bf16[4,64,1024]{2,1,0:T(8,128)(2,1)} %param.29) | copy-start | bytes 1572868
Sparse Core Ops, SparseCore 0:
  37.7 118.1 all-gather.2
  157.6 116.9 all-gather.4
where the time goes:
time: 291 us
  waiting for transfers between devices  135 us (46%)
  blocking collectives  105 us (36%)
  matrix products  29.2 us (10%)
  between operations  14.5 us (5%)
  other arithmetic  4.89 us (2%)
    all_gather x1, waiting for transfers between devices, local(): lax.all_gather(input_slice, 'fsdp', axis=0, tiled=True)  92 us
    all_to_all x1, blocking collectives, sent_to_all(): return lax.all_to_all(copies, axis, split_axis=0, concat_axis=0, tiled=True)  57.7 us
    all_gather x1, waiting for transfers between devices, local(): lax.all_gather(output_slice, 'fsdp', axis=0, tiled=True)  42.5 us
    all_to_all x1, blocking collectives, local(): lax.all_to_all(joined, 'tp', split_axis=1, concat_axis=0, tiled=True)  26 us
    all_to_all x1, blocking collectives, local(): lax.all_to_all(merged_output, 'tp', split_axis=1, concat_axis=0, tiled=True)  21.3 us
    dot_general x1, matrix products, local(): jnp.dot(columns, lax.all_gather(input_slice, 'fsdp', axis=0, tiled=True),...  11.4 us
    dot_general x1, matrix products, local(): jnp.dot(columns, lax.all_gather(output_slice, 'fsdp', axis=0, tiled=True)...  8.16 us
  transfers between devices with their start and end apart: 2, of which 2 were waited for; matrix products, arithmetic and copies ran while one was open for 8% of the time, Pallas kernels for 0%

commit v1 on v0

--- a/solution.py
+++ b/solution.py
@@ -161,7 +161,9 @@
     columns = flat_heads
     low_rank_delta = jnp.dot(
         columns,
-        lax.all_gather(output_slice, "fsdp", axis=0, tiled=True),
+        jnp.concatenate(
+            lax.all_to_all(jnp.stack([output_slice] * lax.axis_size("fsdp")), "fsdp", 0, 0), axis=0
+        ),
         preferred_element_type=jnp.float32,
     )
     low_rank_delta = low_rank_delta.reshape(seq_count, step_count, -1)

time: 291 us -> 426 us (1.46)
  waiting for transfers between devices: 135 us -> 293 us
  blocking collectives: 105 us -> 60.1 us
  starting transfers between devices: 0.04 us -> 12.3 us
  local copies, waits for them, and re-layouts: 2.46 us -> 11.9 us
    all_to_all x0 -> x2, waiting for transfers between devices: none -> 183 us  [the longest x1 183 us: local(): lax.all_to_all(jnp.stack([output_slice] * lax.axis_size('fsdp')), 'fsdp',...]
    all_gather x1 -> x0, waiting for transfers between devices: 42.5 us -> none  [local(): lax.all_gather(output_slice, 'fsdp', axis=0, tiled=True)]
    all_to_all x1, blocking collectives: 57.7 us -> 34.1 us  [sent_to_all(): return lax.all_to_all(copies, axis, split_axis=0, concat_axis=0, tiled=True)]
    all_to_all x1 -> x0, blocking collectives: 21.3 us -> none  [local(): lax.all_to_all(merged_output, 'tp', split_axis=1, concat_axis=0, tiled=True)]
    all_gather x1, waiting for transfers between devices: 92 us -> 110 us  [local(): lax.all_gather(input_slice, 'fsdp', axis=0, tiled=True)]
    all_to_all x0 -> x2, starting transfers between devices: none -> 12.3 us  [the longest x1 7.9 us: local(): lax.all_to_all(jnp.stack([output_slice] * lax.axis_size('fsdp')), 'fsdp',...]
    another operation x0 -> x1, local copies, waits for them, and re-layouts: none -> 6.85 us  [local(): jnp.stack([output_slice] * lax.axis_size('fsdp'))]
  transfers between devices with their start and end apart: 2 -> 3, of which waited for: 2 -> 2; matrix products, arithmetic and copies ran while one was open for 8% -> 6% of each run, Pallas kernels for 0% -> 0%
where the time goes in v1:
time: 426 us
  waiting for transfers between devices  293 us (69%)
  blocking collectives  60.1 us (14%)
  matrix products  29.2 us (7%)
  between operations  14.5 us (3%)
  starting transfers between devices  12.3 us (3%)
  local copies, waits for them, and re-layouts  11.9 us (3%)
  other arithmetic  4.9 us (1%)
    all_to_all x1, waiting for transfers between devices, local(): lax.all_to_all(jnp.stack([output_slice] * lax.axis_size('fsdp')), 'fsdp',...  183 us
    all_gather x1, waiting for transfers between devices, local(): lax.all_gather(input_slice, 'fsdp', axis=0, tiled=True)  110 us
    all_to_all x1, blocking collectives, sent_to_all(): return lax.all_to_all(copies, axis, split_axis=0, concat_axis=0, tiled=True)  34.1 us
    all_to_all x1, blocking collectives, local(): lax.all_to_all(joined, 'tp', split_axis=1, concat_axis=0, tiled=True)  26 us
    dot_general x1, matrix products, local(): jnp.dot(columns, lax.all_gather(input_slice, 'fsdp', axis=0, tiled=True),...  11.4 us
  transfers between devices with their start and end apart: 3, of which 2 were waited for; matrix products, arithmetic and copies ran while one was open for 6% of the time, Pallas kernels for 0%

profile of v1, /device:TPU:1, one launch (start us, length us, event | category | flops | bytes accessed | tf_op | source)
XLA Modules:
  0.0 425.5 jit_solution(3097506989165707831)
XLA Ops:
  6.5 0.0 copy-start
  7.3 2.0 fusion.5
  9.3 0.1 copy.121
  9.4 0.9 fusion.29
  10.3 1.1 fusion.28
  11.4 0.1 copy_bitcast_fusion.2
  11.5 0.1 pad_maximum_fusion
  11.6 0.0 copy-start.5
  11.6 26.0 %all_to_all.42 = bf16[64,8,1280]{2,0,1:T(8,128)(2,1)} all-to-all(bf16[64,8,1280]{2,0,1:T(8,128)(2,1)S(1)} %pad_maximum_fusion), channel_id=1, replica_groups=mesh['fsdp'=16,'tp'=8] {'tp'}, dimensions={1} | all-to-all | bytes 2621440 | tf_op jit(solution)/shard_map/all_to_all | solution.py:128
  37.6 0.0 all-gather.2.cloned.1.call-update
  37.6 0.0 copy-done.5
  37.6 1.7 fusion.4
  39.3 0.0 copy-start.9
  39.3 0.0 copy-start.2
  39.3 1.1 copy.120
  40.4 4.4 %all-to-all-start.2 = ((bf16[64,8,1024]{2,0,1:T(8,128)(2,1)}), bf16[64,8,1024]{2,0,1:T(8,128)(2,1)}, u32[]{:S(2)}, u32[]{:S(2)}) async-start(bf16[64,8,1024]{2,0,1:T(8,128)(2,1)} %bitcast.132), calls=%async_computation.2 | async-start | bytes 2097152 | tf_op jit(solution)/shard_map/all_to_all | solution.py:129
  44.8 0.0 copy-start.3
  44.8 0.1 iota_compare_fusion
  44.9 1.2 fusion.6
  46.1 0.3 multiply_cosine_fusion
  46.4 1.5 fusion.8
  47.9 110.1 %all-gather.2.cloned.1.call-done = bf16[8192,1280]{1,0:T(8,128)(2,1)} async-done(((bf16[512,1280]{1,0:T(8,128)(2,1)}), bf16[8192,1280]{1,0:T(8,128)(2,1)}) %all-gather.2.cloned.1.call-update) | async-done | bytes 20971536 | tf_op jit(solution)/shard_map/all_gather | solution.py:139
  158.0 11.4 %fusion = f32[32,4,1280]{2,0,1:T(8,128)S(1)} fusion(bf16[8192,1280]{1,0:T(8,128)(2,1)} %all-gather.2.cloned.1.call-done, bf16[32,4,8192]{2,1,0:T(4,128)(2,1)S(1)} %fusion.8), kind=kOutput, calls=%fused_computation | convolution fusion | flops 2684354560 | bytes 23724032 | tf_op jit(solution)/shard_map/dot_general | solution.py:137
  169.4 0.1 slice.29
  169.4 0.1 fusion.46
  169.5 0.1 copy.103
  169.6 0.1 fusion.49
  169.9 0.0 copy-start.4
  169.9 0.2 slice_negate_fusion
  170.1 0.2 fusion.38
  170.3 1.3 fusion.66
  171.6 0.4 copy-done.4
  172.0 1.6 fusion.65
  173.6 0.3 fusion.39
  173.9 0.8 fusion.15
  174.7 0.8 fusion.18
  175.6 0.4 fusion.22
  175.9 0.1 reshape.202
  176.0 0.1 copy.86
  176.1 0.0 all-to-all-done.2
  176.1 0.3 broadcast_in_dim.26
  176.3 34.1 %all_to_all.43 = bf16[8,32,4,1024]{3,1,2,0:T(8,128)(2,1)} all-to-all(bf16[8,32,4,1024]{3,1,2,0:T(8,128)(2,1)S(1)} %broadcast_in_dim.26), channel_id=1, replica_groups=mesh['fsdp'=16,'tp'=8] {'tp'}, dimensions={0} | all-to-all | bytes 4194304 | tf_op jit(solution)/shard_map/all_to_all | solution.py:16
  210.5 6.8 %stack.5 = bf16[16,512,1024]{2,1,0:T(8,128)(2,1)} broadcast(bf16[512,1024]{1,0:T(8,128)(2,1)} %bitcast.35), dimensions={1,2} | broadcast | bytes 17825792 | tf_op jit(solution)/shard_map/stack | solution.py:165
  217.3 7.9 %all-to-all-start.3 = ((bf16[16,512,1024]{2,1,0:T(8,128)(2,1)}), bf16[16,512,1024]{2,1,0:T(8,128)(2,1)}, u32[]{:S(2)}, u32[]{:S(2)}) async-start(bf16[16,512,1024]{2,1,0:T(8,128)(2,1)} %stack.5), calls=%async_computation.3 | async-start | bytes 33554432 | tf_op jit(solution)/shard_map/all_to_all | solution.py:165
  225.2 1.8 copy.102
  227.1 182.5 %all-to-all-done.3 = bf16[16,512,1024]{2,1,0:T(8,128)(2,1)} async-done(((bf16[16,512,1024]{2,1,0:T(8,128)(2,1)}), bf16[16,512,1024]{2,1,0:T(8,128)(2,1)}, u32[]{:S(2)}, u32[]{:S(2)}) %all-to-all-start.3) | async-done | bytes 16777248 | tf_op jit(solution)/shard_map/all_to_all | solution.py:165
  409.6 8.2 %convolution_convert_fusion = bf16[32,4,1024]{2,0,1:T(8,128)(2,1)S(1)} fusion(bf16[32,4,8192]{2,0,1:T(8,128)(2,1)S(1)} %bitcast.127, bf16[8192,1024,1]{1,0,2:T(8,128)(2,1)} %bitcast.37), kind=kOutput, calls=%fused_computation.27 | convolution fusion | flops 2147614720 | bytes 19136512 | tf_op jit(solution)/shard_map/dot_general | solution.py:162
  417.7 0.9 copy.89
  (26 shorter events, 0.2 us)
Async XLA Ops:
  6.5 2.9 copy-start
  6.5 151.4 %all-gather.2.cloned.1.call-start = ((), (), s32[]{:S(2)}) async-start(), calls=%async_computation.4 | async-start | bytes 22282240 | tf_op jit(solution)/shard_map/all_gather | solution.py:139
  7.3 2.1 copy-start.6
  7.3 3.0 copy-start.7
  11.6 26.0 %copy-start.5 = (bf16[64,8192]{1,0:T(8,128)(2,1)S(1)}, bf16[64,8192]{1,0:T(8,128)(2,1)}, u32[]{:S(2)}) copy-start(bf16[64,8192]{1,0:T(8,128)(2,1)} %param.23) | copy-start | bytes 3145732
  39.3 5.5 %copy-start.9 = (s32[32]{0:T(128)S(1)}, s32[32]{0:T(128)}, u32[]{:S(2)}) copy-start(s32[32]{0:T(128)} %param.33) | copy-start | bytes 388
  39.3 5.6 %copy-start.2 = (bf16[32,4,8192]{2,1,0:T(4,128)(2,1)S(1)}, bf16[32,4,8192]{2,1,0:T(4,128)(2,1)}, u32[]{:S(2)}) copy-start(bf16[32,4,8192]{2,1,0:T(4,128)(2,1)} %param.18) | copy-start | bytes 6291460
  40.4 6.1 %copy-start.8 = (f32[8192]{0:T(1024)S(1)}, f32[8192]{0:T(1024)}, u32[]{:S(2)}) copy-start(f32[8192]{0:T(1024)} %param.19) | copy-start | bytes 98308
  40.4 135.7 %all-to-all-start.2 = ((bf16[64,8,1024]{2,0,1:T(8,128)(2,1)}), bf16[64,8,1024]{2,0,1:T(8,128)(2,1)}, u32[]{:S(2)}, u32[]{:S(2)}) async-start(bf16[64,8,1024]{2,0,1:T(8,128)(2,1)} %bitcast.132), calls=%async_computation.2 | async-start | bytes 2097152 | tf_op jit(solution)/shard_map/all_to_all | solution.py:129
  44.8 1.7 copy-start.3
  169.9 2.2 copy-start.4
  172.0 2.7 copy-start.10
  217.3 192.2 %all-to-all-start.3 = ((bf16[16,512,1024]{2,1,0:T(8,128)(2,1)}), bf16[16,512,1024]{2,1,0:T(8,128)(2,1)}, u32[]{:S(2)}, u32[]{:S(2)}) async-start(bf16[16,512,1024]{2,1,0:T(8,128)(2,1)} %stack.5), calls=%async_computation.3 | async-start | bytes 33554432 | tf_op jit(solution)/shard_map/all_to_all | solution.py:165
  409.6 9.1 %copy-start.1 = (bf16[4,64,1024]{2,1,0:T(8,128)(2,1)S(1)}, bf16[4,64,1024]{2,1,0:T(8,128)(2,1)}, u32[]{:S(2)}) copy-start(bf16[4,64,1024]{2,1,0:T(8,128)(2,1)} %param.27) | copy-start | bytes 1572868
Sparse Core Ops, SparseCore 0:
  37.7 120.2 all-gather.1
